TPU v7x, 128 devices: a whole 4x4x4 slice. The times are simulated.
128 devices in a mesh: img: 8 (over x, core), pos: 16 (over z, y).
Axes of the slice: x: 4, y: 4, z: 4, core: 2. Of those that a mesh axis runs over, the one named last changes fastest.
Arguments:
- features: bfloat16 [16384, 32, 1536], P(('img', 'pos')), may hold values from -6 to 6
- channel_index: int32 [550], replicated, may hold values from 0 to 1535, as said below
- image_counts: int32 [128], P(('img', 'pos')), may hold values from 32 to 128, as said below
Outputs:
- centres: float32 [32, 550], P('pos')
- covars: float32 [32, 550, 550], P('pos')
Inputs may be any that keep to these rules, and one draw needn't show every extreme that they name: `channel_index`: distinct channel numbers. `image_counts`: some device uses all 128 slots and some only a quarter.
All inputs are finite; a program needn't handle non-finite values.
Results may differ from a plain program's by a relative error of at most 0.0003.
Values may be sent and summed in bfloat16 or wider, within the bound.
A program may use at most 128 MiB of HBM per device.

v0:
```python
import jax
import jax.numpy as jnp
from jax import lax
from jax.sharding import PartitionSpec as P

REG = 0.01


def combined_all(value, axis, combine):
    everything = jax.tree.map(lambda part: lax.all_gather(part, axis), value)
    initial = jax.tree.map(lambda part: part[0], everything)

    def lap(k, so_far):
        return combine(so_far, jax.tree.map(lambda part: part[k], everything))

    return lax.fori_loop(1, lax.axis_size(axis), lap, initial)


def moments(received):
    rows = received[:, 0]
    sq_sum = jnp.einsum("ipk,ipl->pkl", rows, rows, preferred_element_type=jnp.float32)
    lin_sum = jnp.sum(rows.astype(jnp.float32), axis=0)
    return (sq_sum, lin_sum)


def body(features, channel_index, image_counts):
    slots = features.shape[0]
    owners = lax.axis_size("pos")
    owned = features.shape[1] // owners
    usable = lax.iota(jnp.int32, slots) < image_counts[0]
    masked = features * usable.astype(jnp.bfloat16)[:, None, None]
    chosen = jnp.take(masked, channel_index, axis=2)
    chosen = chosen.reshape(slots, owners, owned, chosen.shape[2])
    sq_sum, lin_sum = moments(
        lax.all_to_all(chosen, "pos", split_axis=1, concat_axis=0, tiled=True)
    )
    group_total = lax.psum(image_counts.astype(jnp.float32)[0], "pos")
    width = channel_index.shape[0]
    identity_mat = jnp.eye(width, dtype=jnp.float32)
    centre = lin_sum / group_total
    scatter_mat = sq_sum - group_total * centre[:, :, None] * centre[:, None, :]

    def combine(earlier, later):
        count_low, centre_low, scatter_low = earlier
        count_high, centre_high, scatter_high = later
        joined = count_low + count_high
        offset = centre_high - centre_low
        new_centre = centre_low + offset * (count_high / joined)
        weight_pair = count_low * count_high / joined
        new_scatter = (
            scatter_low + scatter_high + weight_pair * offset[:, :, None] * offset[:, None, :]
        )
        return (joined, new_centre, new_scatter)

    total_count, centre, scatter_mat = combined_all(
        (group_total, centre, scatter_mat), "img", combine
    )
    covar = scatter_mat / (total_count - 1.0) + REG * identity_mat
    return (centre, covar)


def solution(mesh):
    placed = (P(("img", "pos"), None, None), P(), P(("img", "pos")))
    return jax.shard_map(
        body,
        mesh=mesh,
        in_specs=placed,
        out_specs=(P("pos", None), P("pos", None, None)),
        check_vma=False,
    )
```

profile of v0, /device:TPU:1, one launch (start us, length us, event | category | flops | bytes accessed | tf_op | source)
XLA Modules:
  0.0 346.5 jit_solution(6363015843126375706)
XLA Ops:
  9.2 17.9 %copy.24 = bf16[128,32,1536]{0,1,2:T(8,128)(2,1)} copy(bf16[128,32,1536]{2,1,0:T(8,128)(2,1)} %param.5) | data formatting | bytes 25165824 | tf_op args[0]
  27.2 10.4 %broadcast_multiply_fusion.1 = bf16[128,32,1536]{0,1,2:T(8,128)(2,1)} fusion(bf16[128,32,1536]{0,1,2:T(8,128)(2,1)} %copy.24, bf16[128]{0:T(256)(128)(2,1)S(1)} %compare_convert_fusion), kind=kLoop, calls=%fused_computation.7 | loop fusion | flops 6291456 | bytes 25166080 | tf_op jit(solution)/shard_map/mul | solution.py:31
  37.6 8.9 %gather_fusion = bf16[550,128,32]{1,2,0:T(8,128)(2,1)} fusion(bf16[128,32,1536]{0,1,2:T(8,128)(2,1)} %broadcast_multiply_fusion.1, s32[1024]{0:T(1024)S(1)} %pad_clamp_fusion), kind=kCustom, calls=%fused_computation | custom fusion | bytes 9013400 | tf_op jit(solution)/shard_map/jit(_take)/gather | solution.py:32
  46.5 4.0 %copy.25 = bf16[128,32,550]{0,2,1:T(8,128)(2,1)S(1)} copy(bf16[128,32,550]{0,1,2:T(8,128)(2,1)} %bitcast.35) | data formatting | bytes 9011200 | tf_op jit(solution)/shard_map/jit(_take)/gather | solution.py:32
  50.5 2.5 broadcast_select_fusion
  53.0 7.9 %copy.26 = bf16[128,16,2,550]{0,2,3,1:T(2,128)(2,1)} copy(bf16[128,16,2,550]{0,3,2,1:T(8,128)(2,1)} %broadcast_select_fusion) | data formatting | bytes 9011200 | tf_op jit(solution)/shard_map/jit(_take)/select_n | solution.py:32
  60.9 8.6 %all-to-all-start = ((bf16[128,16,2,550]{0,2,3,1:T(2,128)(2,1)}), bf16[128,16,2,550]{0,2,3,1:T(2,128)(2,1)}, u32[]{:S(2)}, u32[]{:S(2)}) async-start(bf16[128,16,2,550]{0,2,3,1:T(2,128)(2,1)} %copy.26), calls=%async_computation | async-start | bytes 9011200 | tf_op jit(solution)/shard_map/all_to_all | solution.py:35
  69.6 89.4 %psum.7 = f32[]{:T(128)} all-reduce(f32[]{:T(128)} %bitcast.3), channel_id=1, replica_groups=mesh['img'=8,'pos'=16] {'pos'}, use_global_device_ids=true, to_apply=%region_0.1 | all-reduce | flops 1 | bytes 8 | tf_op jit(solution)/shard_map/psum | solution.py:37
  159.0 5.9 %convert_reduce_fusion = f32[2,550]{0,1:T(8,128)S(1)} fusion(bf16[128,16,2,550]{0,2,3,1:T(2,128)(2,1)} %all-to-all-done), kind=kLoop, calls=%fused_computation.6 | loop fusion | flops 4504500 | bytes 4510000 | tf_op jit(solution)/shard_map/reduce_sum | solution.py:22
  165.0 5.0 %copy.28 = bf16[16,128,1,2,550]{1,0,4,3,2:T(8,128)(2,1)} copy(bf16[16,128,1,2,550]{1,3,4,0,2:T(2,128)(2,1)} %bitcast.11) | data formatting | bytes 9011200 | tf_op jit(solution)/shard_map/all_to_all | solution.py:35
  170.0 5.0 %squeeze.52 = bf16[2048,2,550]{0,2,1:T(8,128)(2,1)} reshape(bf16[16,128,1,2,550]{1,0,4,3,2:T(8,128)(2,1)} %copy.28) | data formatting | bytes 9011200 | tf_op jit(solution)/shard_map/squeeze | solution.py:20
  175.6 8.9 %multiply_subtract_fusion = f32[2,550,550]{2,1,0:T(8,128)} fusion(bf16[2048,2,550]{0,2,1:T(8,128)(2,1)} %squeeze.52, f32[2,550]{1,0:T(2,128)S(1)} %get-tuple-element.200, f32[2,550]{1,0:T(2,128)S(1)} %get-tuple-element.199), kind=kOutput, calls=%fused_computation.9 | convolution fusion | flops 2479289856 | bytes 6934400 | tf_op jit(solution)/shard_map/ipk,ipl->pkl/dot_general | solution.py:21
  187.2 19.4 %all-reduce = f32[8]{0:T(128)S(1)} all-reduce(f32[8]{0:T(128)S(1)} %dynamic-update-slice), channel_id=1, replica_groups=mesh['img'=8,'pos'=16] {'img'}, use_global_device_ids=true, to_apply=%add | all-reduce | flops 8 | bytes 64
  207.9 13.3 %all-gather.2 = f32[8,2,550]{2,1,0:T(2,128)S(1)} all-gather(f32[1,2,550]{2,1,0:T(2,128)S(1)} %bitcast.38), channel_id=2, replica_groups=mesh['img'=8,'pos'=16] {'img'}, dimensions={0}, use_global_device_ids=true | all-gather | bytes 39600 | tf_op jit(solution)/shard_map/all_gather | solution.py:10
  221.2 76.9 %all-gather.5.cloned.1.call-done = f32[16,550,550]{2,1,0:T(8,128)} async-done(((f32[2,550,550]{2,1,0:T(8,128)}), f32[16,550,550]{2,1,0:T(8,128)}) %all-gather.5.cloned.1.call-update) | async-done | bytes 19360016 | tf_op jit(solution)/shard_map/all_gather | solution.py:10
  300.0 33.8 %while.19 = (s32[]{:T(128)}, f32[]{:T(128)}, f32[2,550]{1,0:T(2,128)S(1)}, f32[2,550,550]{2,1,0:T(8,128)S(1)}, f32[8]{0:T(128)S(1)}, /*index=5*/f32[8,2,550]{2,1...) while((s32[]{:T(128)}, f32[]{:T(128)}, f32[2,550]{1,0:T(2,128)S(1)}, ...), condition=%wide.region_3.4_spmd, body=%wide.region_2.3_spmd.sunk | while | flops 1819409 | bytes 7299827 | solution.py:16
  302.4 2.5 fusion.6
  307.2 2.5 fusion.6
  312.1 2.5 fusion.6
  316.9 2.5 fusion.6
  321.7 2.5 fusion.6
  326.5 2.5 fusion.6
  331.4 2.5 fusion.6
  333.9 5.8 %fusion.1 = f32[2,550,550]{2,0,1:T(2,128)} fusion(f32[2,550,550]{2,1,0:T(8,128)S(1)} %get-tuple-element.181, f32[550,550]{1,0:T(8,128)} %fusion.2, f32[]{:T(128)S(6)} %sub.17), kind=kLoop, calls=%fused_computation.11 | loop fusion | flops 1210000 | bytes 6050004 | tf_op jit(solution)/shard_map/add | solution.py:58
  (40 shorter events, 12.3 us)
Async XLA Ops:
  60.9 98.1 %all-to-all-start = ((bf16[128,16,2,550]{0,2,3,1:T(2,128)(2,1)}), bf16[128,16,2,550]{0,2,3,1:T(2,128)(2,1)}, u32[]{:S(2)}, u32[]{:S(2)}) async-start(bf16[128,16,2,550]{0,2,3,1:T(2,128)(2,1)} %copy.26), calls=%async_computation | async-start | bytes 9011200 | tf_op jit(solution)/shard_map/all_to_all | solution.py:35
  69.6 228.5 %all-gather.5.cloned.1.call-start = ((), (), s32[]{:S(2)}) async-start(), calls=%async_computation.1 | async-start | bytes 25436160 | tf_op jit(solution)/shard_map/all_gather | solution.py:10
  184.6 0.7 copy-start.1
  333.8 5.8 %copy-start = (f32[2,550]{1,0:T(2,128)}, f32[2,550]{1,0:T(2,128)S(1)}, u32[]{:S(2)}) copy-start(f32[2,550]{1,0:T(2,128)S(1)} %get-tuple-element.178) | copy-start | bytes 13204
Sparse Core Ops, SparseCore 0:
  184.7 113.2 all-gather.4
where the time goes:
time: 348 us; the launch traced here: 346 us
  blocking collectives  122 us (35%)
  waiting for transfers between devices  76.9 us (22%)
  local copies, waits for them, and re-layouts  57.5 us (17%)
  other arithmetic  45.2 us (13%)
  between operations  14.8 us (4%)
  loops' own time  12.4 us (4%)
  matrix products  8.93 us (3%)
  starting transfers between devices  8.68 us (2%)
    psum x1, blocking collectives, body(): group_total = lax.psum(image_counts.astype(jnp.float32)[0], 'pos')  89.4 us
    all_gather x1, waiting for transfers between devices, combined_all(): everything = jax.tree.map(lambda part: lax.all_gather(part, axis), value)  76.9 us
    unnamed x8, local copies, waits for them, and re-layouts  20.6 us
    unnamed x1, blocking collectives  19.4 us
    add x7, other arithmetic, combine(): scatter_low + scatter_high  17.2 us
    all_gather x1, blocking collectives, combined_all(): everything = jax.tree.map(lambda part: lax.all_gather(part, axis), value)  13.3 us
    gather x2, local copies, waits for them, and re-layouts, body(): chosen = jnp.take(masked, channel_index, axis=2)  13 us
    another operation x1, loops' own time, combined_all(): return lax.fori_loop(1, lax.axis_size(axis), lap, initial)  12.4 us
  transfers between devices with their start and end apart: 2, of which 1 were waited for; matrix products, arithmetic and copies ran while one was open for 1% of the time, Pallas kernels for 0%

commit v1 on v0

--- a/solution.py
+++ b/solution.py
@@ -1,9 +1,17 @@
+import functools
 import jax
 import jax.numpy as jnp
 from jax import lax
 from jax.sharding import PartitionSpec as P
 
 REG = 0.01
+
+
+def build_islands(v0, axis_tag):
+    return lax.all_gather(v0, axis_name=axis_tag).sum(axis=0)
+
+
+apply_the_bench = functools.partial(build_islands, axis_tag="pos")
 
 
 def combined_all(value, axis, combine):
@@ -34,7 +42,7 @@
     sq_sum, lin_sum = moments(
         lax.all_to_all(chosen, "pos", split_axis=1, concat_axis=0, tiled=True)
     )
-    group_total = lax.psum(image_counts.astype(jnp.float32)[0], "pos")
+    group_total = apply_the_bench(image_counts.astype(jnp.float32)[0])
     width = channel_index.shape[0]
     identity_mat = jnp.eye(width, dtype=jnp.float32)
     centre = lin_sum / group_total

time: 348 us -> 350 us (level)
    psum x1 -> x0, blocking collectives: 89.4 us -> none  [body(): group_total = lax.psum(image_counts.astype(jnp.float32)[0], 'pos')]
    unnamed x1 -> x2, blocking collectives: 19.4 us -> 107 us
    unnamed x8 -> x12, local copies, waits for them, and re-layouts: 20.6 us -> 21.2 us
where the time goes in v1:
time: 350 us; the launch traced here: 348 us
  blocking collectives  120 us (34%)
  waiting for transfers between devices  76.9 us (22%)
  local copies, waits for them, and re-layouts  58.3 us (17%)
  other arithmetic  46.6 us (13%)
  between operations  14.8 us (4%)
  loops' own time  13.7 us (4%)
  matrix products  8.94 us (3%)
  starting transfers between devices  8.82 us (3%)
    unnamed x2, blocking collectives  107 us
    all_gather x1, waiting for transfers between devices, combined_all(): everything = jax.tree.map(lambda part: lax.all_gather(part, axis), value)  76.9 us
    unnamed x12, local copies, waits for them, and re-layouts  21.2 us
    add x7, other arithmetic, combine(): scatter_low + scatter_high  17.2 us
    another operation x1, loops' own time, combined_all(): return lax.fori_loop(1, lax.axis_size(axis), lap, initial)  13.7 us
    all_gather x1, blocking collectives, combined_all(): everything = jax.tree.map(lambda part: lax.all_gather(part, axis), value)  13.3 us
    gather x2, local copies, waits for them, and re-layouts, body(): chosen = jnp.take(masked, channel_index, axis=2)  13 us
    mul x1, other arithmetic, body(): masked = features * usable.astype(jnp.bfloat16)[:, None, None]  10.4 us
  transfers between devices with their start and end apart: 2, of which 1 were waited for; matrix products, arithmetic and copies ran while one was open for 1% of the time, Pallas kernels for 0%

profile of v1, /device:TPU:1, one launch (start us, length us, event | category | flops | bytes accessed | tf_op | source)
XLA Modules:
  0.0 348.2 jit_solution(329749366503837087)
XLA Ops:
  9.2 17.9 %copy.24 = bf16[128,32,1536]{0,1,2:T(8,128)(2,1)} copy(bf16[128,32,1536]{2,1,0:T(8,128)(2,1)} %param.5) | data formatting | bytes 25165824 | tf_op args[0]
  27.2 10.4 %broadcast_multiply_fusion.1 = bf16[128,32,1536]{0,1,2:T(8,128)(2,1)} fusion(bf16[128,32,1536]{0,1,2:T(8,128)(2,1)} %copy.24, bf16[128]{0:T(256)(128)(2,1)S(1)} %compare_convert_fusion), kind=kLoop, calls=%fused_computation.7 | loop fusion | flops 6291456 | bytes 25166080 | tf_op jit(solution)/shard_map/mul | solution.py:39
  37.6 9.0 %gather_fusion = bf16[550,128,32]{1,2,0:T(8,128)(2,1)} fusion(bf16[128,32,1536]{0,1,2:T(8,128)(2,1)} %broadcast_multiply_fusion.1, s32[1024]{0:T(1024)S(1)} %pad_clamp_fusion), kind=kCustom, calls=%fused_computation | custom fusion | bytes 9013400 | tf_op jit(solution)/shard_map/jit(_take)/gather | solution.py:40
  46.5 4.0 %copy.25 = bf16[128,32,550]{0,2,1:T(8,128)(2,1)S(1)} copy(bf16[128,32,550]{0,1,2:T(8,128)(2,1)} %bitcast.35) | data formatting | bytes 9011200 | tf_op jit(solution)/shard_map/jit(_take)/gather | solution.py:40
  50.6 2.5 broadcast_select_fusion
  53.1 7.9 %copy.26 = bf16[128,16,2,550]{0,2,3,1:T(2,128)(2,1)} copy(bf16[128,16,2,550]{0,3,2,1:T(8,128)(2,1)} %broadcast_select_fusion) | data formatting | bytes 9011200 | tf_op jit(solution)/shard_map/jit(_take)/select_n | solution.py:40
  60.9 8.8 %all-to-all-start = ((bf16[128,16,2,550]{0,2,3,1:T(2,128)(2,1)}), bf16[128,16,2,550]{0,2,3,1:T(2,128)(2,1)}, u32[]{:S(2)}, u32[]{:S(2)}) async-start(bf16[128,16,2,550]{0,2,3,1:T(2,128)(2,1)} %copy.26), calls=%async_computation | async-start | bytes 9011200 | tf_op jit(solution)/shard_map/all_to_all | solution.py:43
  71.1 87.5 %all-reduce = f32[16]{0:T(128)S(1)} all-reduce(f32[16]{0:T(128)S(1)} %convert_dynamic-update-slice_fusion), channel_id=1, replica_groups=mesh['img'=8,'pos'=16] {'pos'}, use_global_device_ids=true, to_apply=%add | all-reduce | flops 16 | bytes 128
  159.2 5.9 %convert_reduce_fusion = f32[2,550]{0,1:T(8,128)S(1)} fusion(bf16[128,16,2,550]{0,2,3,1:T(2,128)(2,1)} %all-to-all-done), kind=kLoop, calls=%fused_computation.6 | loop fusion | flops 4504500 | bytes 4510000 | tf_op jit(solution)/shard_map/reduce_sum | solution.py:30
  165.3 5.0 %copy.28 = bf16[16,128,1,2,550]{1,0,4,3,2:T(8,128)(2,1)} copy(bf16[16,128,1,2,550]{1,3,4,0,2:T(2,128)(2,1)} %bitcast.11) | data formatting | bytes 9011200 | tf_op jit(solution)/shard_map/all_to_all | solution.py:43
  170.3 5.0 %squeeze.48 = bf16[2048,2,550]{0,2,1:T(8,128)(2,1)} reshape(bf16[16,128,1,2,550]{1,0,4,3,2:T(8,128)(2,1)} %copy.28) | data formatting | bytes 9011200 | tf_op jit(solution)/shard_map/squeeze | solution.py:28
  175.9 8.9 %multiply_subtract_fusion = f32[2,550,550]{2,1,0:T(8,128)} fusion(bf16[2048,2,550]{0,2,1:T(8,128)(2,1)} %squeeze.48, f32[2,550]{1,0:T(2,128)S(1)} %get-tuple-element.200, f32[2,550]{1,0:T(2,128)S(1)} %get-tuple-element.199), kind=kOutput, calls=%fused_computation.9 | convolution fusion | flops 2479289856 | bytes 6934400 | tf_op jit(solution)/shard_map/ipk,ipl->pkl/dot_general | solution.py:29
  187.5 19.4 %all-reduce.1 = f32[8]{0:T(128)S(1)} all-reduce(f32[8]{0:T(128)S(1)} %dynamic-update-slice.1), channel_id=1, replica_groups=mesh['img'=8,'pos'=16] {'img'}, use_global_device_ids=true, to_apply=%add.1 | all-reduce | flops 8 | bytes 64
  208.2 13.3 %all-gather.2 = f32[8,2,550]{2,1,0:T(2,128)S(1)} all-gather(f32[1,2,550]{2,1,0:T(2,128)S(1)} %bitcast.38), channel_id=2, replica_groups=mesh['img'=8,'pos'=16] {'img'}, dimensions={0}, use_global_device_ids=true | all-gather | bytes 39600 | tf_op jit(solution)/shard_map/all_gather | solution.py:18
  221.5 76.9 %all-gather.5.cloned.1.call-done = f32[16,550,550]{2,1,0:T(8,128)} async-done(((f32[2,550,550]{2,1,0:T(8,128)}), f32[16,550,550]{2,1,0:T(8,128)}) %all-gather.5.cloned.1.call-update) | async-done | bytes 19360016 | tf_op jit(solution)/shard_map/all_gather | solution.py:18
  300.3 35.2 %while.19 = (s32[]{:T(128)}, f32[]{:T(128)}, f32[2,550]{1,0:T(2,128)S(1)}, f32[2,550,550]{2,1,0:T(8,128)S(1)}, f32[8]{0:T(128)S(1)}, /*index=5*/f32[8,2,550]{2,1...) while((s32[]{:T(128)}, f32[]{:T(128)}, f32[2,550]{1,0:T(2,128)S(1)}, ...), condition=%wide.region_3.4_spmd, body=%wide.region_2.3_spmd.sunk | while | flops 1819409 | bytes 7299827 | solution.py:24
  302.9 2.5 fusion.6
  307.9 2.5 fusion.6
  313.0 2.5 fusion.6
  318.0 2.5 fusion.6
  323.0 2.5 fusion.6
  328.1 2.5 fusion.6
  333.1 2.5 fusion.6
  335.6 5.8 %fusion.1 = f32[2,550,550]{2,0,1:T(2,128)} fusion(f32[2,550,550]{2,1,0:T(8,128)S(1)} %get-tuple-element.181, f32[550,550]{1,0:T(8,128)} %fusion.2, f32[]{:T(128)S(6)} %sub.17), kind=kLoop, calls=%fused_computation.11 | loop fusion | flops 1210000 | bytes 6050004 | tf_op jit(solution)/shard_map/add | solution.py:66
  (46 shorter events, 14.4 us)
Async XLA Ops:
  60.9 8.8 %copy-start.2 = (u32[128]{0:T(128)S(1)}, u32[128]{0:T(128)}, u32[]{:S(2)}) copy-start(u32[128]{0:T(128)} %constant.64) | copy-start | bytes 1540
  60.9 98.3 %all-to-all-start = ((bf16[128,16,2,550]{0,2,3,1:T(2,128)(2,1)}), bf16[128,16,2,550]{0,2,3,1:T(2,128)(2,1)}, u32[]{:S(2)}, u32[]{:S(2)}) async-start(bf16[128,16,2,550]{0,2,3,1:T(2,128)(2,1)} %copy.26), calls=%async_computation | async-start | bytes 9011200 | tf_op jit(solution)/shard_map/all_to_all | solution.py:43
  69.7 228.6 %all-gather.5.cloned.1.call-start = ((), (), s32[]{:S(2)}) async-start(), calls=%async_computation.1 | async-start | bytes 25436160 | tf_op jit(solution)/shard_map/all_gather | solution.py:18
  184.9 0.7 copy-start.1
  335.6 5.8 %copy-start = (f32[2,550]{1,0:T(2,128)}, f32[2,550]{1,0:T(2,128)S(1)}, u32[]{:S(2)}) copy-start(f32[2,550]{1,0:T(2,128)S(1)} %get-tuple-element.178) | copy-start | bytes 13204
Sparse Core Ops, SparseCore 0:
  185.0 113.2 all-gather.4
